TPU v7x, 512 devices: a whole 4x8x8 slice. The times are simulated.
512 devices in a mesh: group: 8 (over y), mesh: 32 (over z, x), comp: 2 (over core).
Axes of the slice: x: 4, y: 8, z: 8, core: 2. Of those that a mesh axis runs over, the one named last changes fastest.
Arguments:
- log_sigma: float32 [2048, 128], P('mesh'), may hold values from -1 to 1
- block_owner: int32 [8, 4096, 1], P('group', 'mesh'), may hold values from 0 to 31; in each aligned block of 128 rows (0 to 127, 128 to 255, ..., all dimensions but the last counted through in order) at most 8 rows name the same one
- block_slot: int32 [8, 4096], P('group', 'mesh'), may hold values from 0 to 63
- coupling: float32 [128, 128], replicated, may hold values from -0.6 to 10, as said below
- sources: float32 [8, 2, 8, 4096, 128], P('group', 'comp', None, 'mesh'), may hold values from -24 to 24
- rcv_cell: int32 [8, 4096], P('group', 'mesh'), may hold values from 0 to 16383
- observed: float32 [8, 2, 8, 4096], P('group', 'comp', None, 'mesh'), may hold values from -6 to 6
Outputs:
- gradient: float32 [2048, 128], P('mesh')
Inputs may be any that keep to these rules, and one draw needn't show every extreme that they name: `block_owner`: in the 128 rows of one device of a group, no owner is named more than 8 times; some owner is named exactly 8 times in some device's rows. `rcv_cell`: A receiver's cell counts from the first cell of the modelling section of the device that holds the receiver's entry. `coupling`: every diagonal entry is 6 or more.
All inputs are finite; a program needn't handle non-finite values.
Results may differ from a plain program's by a relative error of at most 0.0003.
Values sent between devices are 32-bit elements; how exact they have to be, the bound alone decides.
A program may use at most 64 MiB of HBM per device.

v0:
```python
import jax
import jax.numpy as jnp
from jax import lax
from jax.sharding import PartitionSpec as P

CELLS = 128
S = 8
ITERS = 6
omega_freq = 0.8
chain_weight = 1.0


def from_partner(value, axis, distance):
    mask = 2**distance
    pairs = [(source, source ^ mask) for source in range(lax.axis_size(axis))]
    return lax.ppermute(value, axis, pairs)


def with_halo(x, sides, width):
    for axis, dim in sides:
        size, length = (lax.axis_size(axis), x.shape[dim])
        up = [(i, (i + 1) % size) for i in range(size - 1)]
        down = [(j, i) for i, j in up]
        last = lax.slice_in_dim(x, length - width, length, axis=dim)
        initial = lax.slice_in_dim(x, 0, width, axis=dim)
        before = lax.ppermute(last, axis, up)
        after = lax.ppermute(initial, axis, down)
        x = jnp.concatenate([before, x, after], axis=dim)
    return x


def partner(values):
    return from_partner(values, "comp", 0)


def beside(values):
    padded = with_halo(values, (("mesh", 1),), 1)
    return padded[:, :-2] + padded[:, 2:]


def cell_product(values, matrix):
    shaped = values.reshape(values.shape[:-1] + (-1, CELLS))
    product = jnp.einsum("...bj,ij->...bi", shaped, matrix, precision=lax.Precision.HIGHEST)
    return product.reshape(values.shape)


def operate(values, matrix, cross_coef):
    return (
        cell_product(values, matrix) - chain_weight * beside(values) + cross_coef * partner(values)
    )


def relax(right, matrix, cross_coef, inverse_diag, apply_op):
    state = jnp.zeros_like(right)
    for iteration in range(ITERS):
        state = state + inverse_diag * (right - apply_op(state, matrix, cross_coef))
    return state


def local(log_sigma, block_owner, block_slot, coupling, sources, rcv_cell, observed):
    owners = block_owner[0, :, 0]
    slots = block_slot[0]
    blocks_dev = owners.shape[0]
    inv_rows = log_sigma.shape[0]
    targets = owners * inv_rows + slots
    gathered = lax.all_gather(log_sigma, "mesh", axis=0, tiled=True)
    model_part = jnp.take(gathered, targets, axis=0)
    sigmas = jnp.exp(model_part).reshape(-1)
    receivers = rcv_cell[0]
    parity = (2 * lax.axis_index("comp") - 1).astype(jnp.float32)
    forward_coef = parity * omega_freq * sigmas
    inverse_diag = jnp.tile(1.0 / jnp.diagonal(coupling), blocks_dev)
    right = sources.reshape(S, -1)
    field_now = relax(right, coupling, forward_coef, inverse_diag, operate)
    field_other = partner(field_now)
    misfit = field_now[:, receivers] - observed[0, 0]
    adjoint_src = jnp.zeros_like(right).at[:, receivers].add(misfit)
    adjoint = relax(adjoint_src, coupling.T, -forward_coef, inverse_diag, operate)
    weighted = -parity * jnp.sum(adjoint * field_other, axis=0)
    partial_rows = (omega_freq * sigmas * weighted).reshape(blocks_dev, CELLS)
    inside_rows = (targets >= 0) & (targets < inv_rows * lax.axis_size("mesh"))
    kept_rows = jnp.where(inside_rows, targets, inv_rows * lax.axis_size("mesh"))
    owned = lax.psum_scatter(
        jnp.zeros((inv_rows * lax.axis_size("mesh"), CELLS), jnp.float32)
        .at[kept_rows]
        .add(partial_rows, mode="drop"),
        "mesh",
        scatter_dimension=0,
        tiled=True,
    )
    return lax.psum(owned, ("group", "comp"))


def solution(mesh):
    in_specs = (
        P("mesh", None),
        P("group", "mesh", None),
        P("group", "mesh"),
        P(),
        P("group", "comp", None, "mesh", None),
        P("group", "mesh"),
        P("group", "comp", None, "mesh"),
    )
    out_specs = P("mesh", None)
    return jax.shard_map(local, mesh=mesh, in_specs=in_specs, out_specs=out_specs, check_vma=False)
```

profile of v0, /device:TPU:32, one launch (start us, length us, event | category | flops | bytes accessed | tf_op | source)
XLA Modules:
  0.0 532.8 jit_solution(2460921501740615536)
XLA Ops:
  6.5 0.7 all-gather.2.cloned.1.call-update
  7.3 1.3 collective-permute-start.1
  8.6 4.5 collective-permute-start
  13.2 1.9 collective-permute-start.2
  15.2 1.2 gather_fusion.1
  17.0 0.7 compare_and_fusion
  17.7 0.7 fusion.121
  18.4 78.7 %all-gather.2.cloned.1.call-done = f32[2048,128]{1,0:T(8,128)} async-done(((f32[64,128]{1,0:T(8,128)}), f32[2048,128]{1,0:T(8,128)}) %all-gather.2.cloned.1.call-update) | async-done | bytes 1048592 | tf_op jit(solution)/shard_map/all_gather | solution.py:66
  97.1 1.9 gather_fusion
  99.1 1.7 fusion.8
  100.8 1.9 collective-permute-start.5
  102.8 1.3 collective-permute-start.4
  104.1 4.5 collective-permute-start.3
  108.6 1.3 collective-permute-done.3
  109.9 1.9 fusion.10
  111.9 1.9 collective-permute-start.8
  113.9 1.3 collective-permute-start.7
  115.2 4.8 collective-permute-start.6
  120.0 0.6 convolution_bitcast_fusion.8
  120.6 0.7 collective-permute-done.6
  121.8 1.9 collective-permute-start.11
  123.8 1.3 collective-permute-start.10
  125.1 4.8 collective-permute-start.9
  129.9 1.3 collective-permute-done.9
  131.2 0.9 fusion.14
  132.1 1.9 collective-permute-start.14
  134.1 1.3 collective-permute-start.13
  135.4 4.8 collective-permute-start.12
  140.2 0.6 convolution_bitcast_fusion.6
  140.8 0.7 collective-permute-done.12
  142.1 1.9 collective-permute-start.17
  144.8 1.3 collective-permute-start.16
  146.1 5.5 %collective-permute-start.15 = (f32[8,1]{1,0:T(8,128)S(1)}, f32[8,1]{1,0:T(8,128)S(1)}, u32[]{:S(2)}, u32[]{:S(2)}) collective-permute-start(f32[8,1]{1,0:T(8,128)S(1)} %get-tuple-element.17), channel_id=1, source_target_pairs={{0,2},{2,4},{4,6},{6,8},{8,10},{10,12},{12,14},{14,16},{16,18},{18... | collective-permute-start | bytes 104 | tf_op jit(solution)/shard_map/ppermute | solution.py:26
  151.6 1.3 collective-permute-done.15
  152.9 1.9 fusion.18
  154.8 5.3 copy.271
  160.1 6.0 %scatter_custom_fusion = f32[8,16384]{0,1:T(8,128)} fusion(s32[128]{0:T(128)S(1)} %fusion.122, f32[]{:T(128)} %constant.12.clone.1, f32[1,1,8,128]{2,3,1,0:T(8,128)S(1)} %copy.272, f32[8,16384]{0,1:T(8,128)} %copy.271, s32[1024]{0:T(1024)S(1)} %pad_clamp_fusion), kind=kCustom, calls=%fused_computation.15 | custom fusion | flops 2048 | bytes 1118212 | tf_op jit(solution)/shard_map/scatter-add | solution.py:77
  166.1 5.5 %copy.273 = f32[8,16384]{1,0:T(8,128)S(1)} copy(f32[8,16384]{0,1:T(8,128)} %scatter_custom_fusion) | data formatting | bytes 1048576 | tf_op jit(solution)/shard_map/scatter-add | solution.py:77
  172.0 1.9 collective-permute-start.20
  174.0 1.3 collective-permute-start.19
  175.3 6.9 %collective-permute-start.18 = (f32[8,1]{1,0:T(8,128)S(1)}, f32[8,1]{1,0:T(8,128)S(1)}, u32[]{:S(2)}, u32[]{:S(2)}) collective-permute-start(f32[8,1]{1,0:T(8,128)S(1)} %get-tuple-element.15), channel_id=1, source_target_pairs={{0,2},{2,4},{4,6},{6,8},{8,10},{10,12},{12,14},{14,16},{16,18},{18... | collective-permute-start | bytes 104 | tf_op jit(solution)/shard_map/ppermute | solution.py:26
  182.3 1.3 collective-permute-done.18
  183.6 0.7 fusion.50
  184.2 1.9 collective-permute-start.23
  186.2 1.3 collective-permute-start.22
  187.5 6.9 %collective-permute-start.21 = (f32[8,1]{1,0:T(8,128)S(1)}, f32[8,1]{1,0:T(8,128)S(1)}, u32[]{:S(2)}, u32[]{:S(2)}) collective-permute-start(f32[8,1]{1,0:T(8,128)S(1)} %get-tuple-element.13), channel_id=1, source_target_pairs={{0,2},{2,4},{4,6},{6,8},{8,10},{10,12},{12,14},{14,16},{16,18},{18... | collective-permute-start | bytes 104 | tf_op jit(solution)/shard_map/ppermute | solution.py:26
  195.0 0.7 collective-permute-done.21
  196.2 1.9 collective-permute-start.26
  198.2 1.3 collective-permute-start.25
  199.5 6.9 %collective-permute-start.24 = (f32[8,1]{1,0:T(8,128)S(1)}, f32[8,1]{1,0:T(8,128)S(1)}, u32[]{:S(2)}, u32[]{:S(2)}) collective-permute-start(f32[8,1]{1,0:T(8,128)S(1)} %get-tuple-element.11), channel_id=1, source_target_pairs={{0,2},{2,4},{4,6},{6,8},{8,10},{10,12},{12,14},{14,16},{16,18},{18... | collective-permute-start | bytes 104 | tf_op jit(solution)/shard_map/ppermute | solution.py:26
  206.4 1.3 collective-permute-done.24
  207.7 0.7 fusion.38
  208.4 1.9 collective-permute-start.29
  210.3 2.4 collective-permute-start.33
  212.8 1.3 collective-permute-start.28
  214.1 6.9 %collective-permute-start.27 = (f32[8,1]{1,0:T(8,128)S(1)}, f32[8,1]{1,0:T(8,128)S(1)}, u32[]{:S(2)}, u32[]{:S(2)}) collective-permute-start(f32[8,1]{1,0:T(8,128)S(1)} %get-tuple-element.9), channel_id=1, source_target_pairs={{0,2},{2,4},{4,6},{6,8},{8,10},{10,12},{12,14},{14,16},{16,18},{18... | collective-permute-start | bytes 104 | tf_op jit(solution)/shard_map/ppermute | solution.py:26
  221.6 0.7 collective-permute-done.27
  222.8 1.9 collective-permute-start.32
  224.8 1.3 collective-permute-start.31
  226.1 6.9 %collective-permute-start.30 = (f32[8,1]{1,0:T(8,128)S(1)}, f32[8,1]{1,0:T(8,128)S(1)}, u32[]{:S(2)}, u32[]{:S(2)}) collective-permute-start(f32[8,1]{1,0:T(8,128)S(1)} %get-tuple-element.7), channel_id=1, source_target_pairs={{0,2},{2,4},{4,6},{6,8},{8,10},{10,12},{12,14},{14,16},{16,18},{18... | collective-permute-start | bytes 104 | tf_op jit(solution)/shard_map/ppermute | solution.py:26
  233.6 0.7 collective-permute-done.30
  234.7 2.1 scatter_custom_fusion.1
  236.8 242.3 %reduce-scatter.2.cloned.1.call-done = f32[64,128]{1,0:T(8,128)} async-done(((f32[2048,128]{1,0:T(8,128)}), f32[64,128]{1,0:T(8,128)}) %reduce-scatter.2.cloned.1.call-update) | async-done | bytes 32784 | tf_op jit(solution)/shard_map/reduce_scatter | solution.py:83
  479.1 46.9 %psum.7 = f32[64,128]{1,0:T(8,128)} all-reduce(f32[64,128]{1,0:T(8,128)} %reduce-scatter.2.cloned.1.call-done), channel_id=1, replica_groups=mesh['group'=8,'mesh'=32,'comp'=2] {'group','comp'}, use_global_device_ids=true, to_apply=%region_4.5 | all-reduce | flops 8192 | bytes 65536 | tf_op jit(solution)/shard_map/psum | solution.py:91
  (66 shorter events, 6.6 us)
Async XLA Ops:
  6.5 8.7 %copy-start = (f32[128,128]{1,0:T(8,128)S(1)}, f32[128,128]{1,0:T(8,128)}, u32[]{:S(2)}) copy-start(f32[128,128]{1,0:T(8,128)} %param.10) | copy-start | bytes 196612
  6.5 114.8 %copy-start.1 = (f32[1,1,8,128,128]{4,3,2,1,0:T(8,128)S(1)}, f32[1,1,8,128,128]{4,3,2,1,0:T(8,128)}, u32[]{:S(2)}) copy-start(f32[1,1,8,128,128]{4,3,2,1,0:T(8,128)} %param.11) | copy-start | bytes 1572868
  6.5 90.6 %all-gather.2.cloned.1.call-start = ((), (), s32[]{:S(2)}) async-start(), calls=%async_computation.1 | async-start | bytes 1081344 | tf_op jit(solution)/shard_map/all_gather | solution.py:66
  7.3 471.8 %reduce-scatter.2.cloned.1.call-start = ((), (), s32[]{:S(2)}) async-start(), calls=%async_computation.2 | async-start | bytes 1081344 | tf_op jit(solution)/shard_map/reduce_scatter | solution.py:83
  7.3 91.8 %collective-permute-start.1 = (f32[8,1]{1,0:T(8,128)S(1)}, f32[8,1]{1,0:T(8,128)S(1)}, u32[]{:S(2)}, u32[]{:S(2)}) collective-permute-start(f32[8,1]{1,0:T(8,128)S(1)} %broadcast.157), channel_id=1, source_target_pairs={{2,0},{4,2},{6,4},{8,6},{10,8},{12,10},{14,12},{16,14},{18,16},{20... | collective-permute-start | bytes 104 | tf_op jit(solution)/shard_map/ppermute | solution.py:27
  8.6 90.5 %collective-permute-start = (f32[8,1]{1,0:T(8,128)S(1)}, f32[8,1]{1,0:T(8,128)S(1)}, u32[]{:S(2)}, u32[]{:S(2)}) collective-permute-start(f32[8,1]{1,0:T(8,128)S(1)} %broadcast.157), channel_id=1, source_target_pairs={{0,2},{2,4},{4,6},{6,8},{8,10},{10,12},{12,14},{14,16},{16,18},{18... | collective-permute-start | bytes 104 | tf_op jit(solution)/shard_map/ppermute | solution.py:26
  13.2 130.8 %copy-start.3 = (s32[1,128]{1,0:T(1,128)S(1)}, s32[1,128]{1,0:T(1,128)}, u32[]{:S(2)}) copy-start(s32[1,128]{1,0:T(1,128)} %param.12) | copy-start | bytes 1540
  13.2 130.8 %copy-start.2 = (f32[1,1,8,128]{3,2,1,0:T(8,128)S(1)}, f32[1,1,8,128]{3,2,1,0:T(8,128)}, u32[]{:S(2)}) copy-start(f32[1,1,8,128]{3,2,1,0:T(8,128)} %param.13) | copy-start | bytes 12292
  13.2 85.8 %collective-permute-start.2 = (f32[8,16384]{1,0:T(8,128)S(1)}, f32[8,16384]{1,0:T(8,128)S(1)}, u32[]{:S(2)}, u32[]{:S(2)}) collective-permute-start(f32[8,16384]{1,0:T(8,128)S(1)} %broadcast.154.clone), channel_id=1, source_target_pairs={{0,1},{1,0},{2,3},{3,2},{4,5},{5,4},{6,7},{7,6},{8,9},{9,8},{10,11... | collective-permute-start | bytes 1572872 | tf_op jit(solution)/shard_map/ppermute | solution.py:16
  100.8 9.2 %collective-permute-start.5 = (f32[8,16384]{1,0:T(8,128)S(1)}, f32[8,16384]{1,0:T(8,128)S(1)}, u32[]{:S(2)}, u32[]{:S(2)}) collective-permute-start(f32[8,16384]{1,0:T(8,128)S(1)} %fusion.8), channel_id=1, source_target_pairs={{0,1},{1,0},{2,3},{3,2},{4,5},{5,4},{6,7},{7,6},{8,9},{9,8},{10,11... | collective-permute-start | bytes 1572872 | tf_op jit(solution)/shard_map/ppermute | solution.py:16
  102.8 5.8 %collective-permute-start.4 = (f32[8,1]{1,0:T(8,128)S(1)}, f32[8,1]{1,0:T(8,128)S(1)}, u32[]{:S(2)}, u32[]{:S(2)}) collective-permute-start(f32[8,1]{1,0:T(8,128)S(1)} %get-tuple-element.26), channel_id=1, source_target_pairs={{2,0},{4,2},{6,4},{8,6},{10,8},{12,10},{14,12},{16,14},{18,16},{20... | collective-permute-start | bytes 104 | tf_op jit(solution)/shard_map/ppermute | solution.py:27
  104.1 5.9 %collective-permute-start.3 = (f32[8,1]{1,0:T(8,128)S(1)}, f32[8,1]{1,0:T(8,128)S(1)}, u32[]{:S(2)}, u32[]{:S(2)}) collective-permute-start(f32[8,1]{1,0:T(8,128)S(1)} %get-tuple-element.25), channel_id=1, source_target_pairs={{0,2},{2,4},{4,6},{6,8},{8,10},{10,12},{12,14},{14,16},{16,18},{18... | collective-permute-start | bytes 104 | tf_op jit(solution)/shard_map/ppermute | solution.py:26
  111.9 9.4 %collective-permute-start.8 = (f32[8,16384]{1,0:T(8,128)S(1)}, f32[8,16384]{1,0:T(8,128)S(1)}, u32[]{:S(2)}, u32[]{:S(2)}) collective-permute-start(f32[8,16384]{1,0:T(8,128)S(1)} %fusion.10), channel_id=1, source_target_pairs={{0,1},{1,0},{2,3},{3,2},{4,5},{5,4},{6,7},{7,6},{8,9},{9,8},{10,11... | collective-permute-start | bytes 1572872 | tf_op jit(solution)/shard_map/ppermute | solution.py:16
  113.9 6.7 %collective-permute-start.7 = (f32[8,1]{1,0:T(8,128)S(1)}, f32[8,1]{1,0:T(8,128)S(1)}, u32[]{:S(2)}, u32[]{:S(2)}) collective-permute-start(f32[8,1]{1,0:T(8,128)S(1)} %get-tuple-element.24), channel_id=1, source_target_pairs={{2,0},{4,2},{6,4},{8,6},{10,8},{12,10},{14,12},{16,14},{18,16},{20... | collective-permute-start | bytes 104 | tf_op jit(solution)/shard_map/ppermute | solution.py:27
  115.2 6.1 %collective-permute-start.6 = (f32[8,1]{1,0:T(8,128)S(1)}, f32[8,1]{1,0:T(8,128)S(1)}, u32[]{:S(2)}, u32[]{:S(2)}) collective-permute-start(f32[8,1]{1,0:T(8,128)S(1)} %get-tuple-element.23), channel_id=1, source_target_pairs={{0,2},{2,4},{4,6},{6,8},{8,10},{10,12},{12,14},{14,16},{16,18},{18... | collective-permute-start | bytes 104 | tf_op jit(solution)/shard_map/ppermute | solution.py:26
  121.8 9.4 %collective-permute-start.11 = (f32[8,16384]{1,0:T(8,128)S(1)}, f32[8,16384]{1,0:T(8,128)S(1)}, u32[]{:S(2)}, u32[]{:S(2)}) collective-permute-start(f32[8,16384]{1,0:T(8,128)S(1)} %fusion.12), channel_id=1, source_target_pairs={{0,1},{1,0},{2,3},{3,2},{4,5},{5,4},{6,7},{7,6},{8,9},{9,8},{10,11... | collective-permute-start | bytes 1572872 | tf_op jit(solution)/shard_map/ppermute | solution.py:16
  123.8 6.1 %collective-permute-start.10 = (f32[8,1]{1,0:T(8,128)S(1)}, f32[8,1]{1,0:T(8,128)S(1)}, u32[]{:S(2)}, u32[]{:S(2)}) collective-permute-start(f32[8,1]{1,0:T(8,128)S(1)} %get-tuple-element.22), channel_id=1, source_target_pairs={{2,0},{4,2},{6,4},{8,6},{10,8},{12,10},{14,12},{16,14},{18,16},{20... | collective-permute-start | bytes 104 | tf_op jit(solution)/shard_map/ppermute | solution.py:27
  125.1 6.1 %collective-permute-start.9 = (f32[8,1]{1,0:T(8,128)S(1)}, f32[8,1]{1,0:T(8,128)S(1)}, u32[]{:S(2)}, u32[]{:S(2)}) collective-permute-start(f32[8,1]{1,0:T(8,128)S(1)} %get-tuple-element.21), channel_id=1, source_target_pairs={{0,2},{2,4},{4,6},{6,8},{8,10},{10,12},{12,14},{14,16},{16,18},{18... | collective-permute-start | bytes 104 | tf_op jit(solution)/shard_map/ppermute | solution.py:26
  132.1 9.4 %collective-permute-start.14 = (f32[8,16384]{1,0:T(8,128)S(1)}, f32[8,16384]{1,0:T(8,128)S(1)}, u32[]{:S(2)}, u32[]{:S(2)}) collective-permute-start(f32[8,16384]{1,0:T(8,128)S(1)} %fusion.14), channel_id=1, source_target_pairs={{0,1},{1,0},{2,3},{3,2},{4,5},{5,4},{6,7},{7,6},{8,9},{9,8},{10,11... | collective-permute-start | bytes 1572872 | tf_op jit(solution)/shard_map/ppermute | solution.py:16
  134.1 6.7 %collective-permute-start.13 = (f32[8,1]{1,0:T(8,128)S(1)}, f32[8,1]{1,0:T(8,128)S(1)}, u32[]{:S(2)}, u32[]{:S(2)}) collective-permute-start(f32[8,1]{1,0:T(8,128)S(1)} %get-tuple-element.20), channel_id=1, source_target_pairs={{2,0},{4,2},{6,4},{8,6},{10,8},{12,10},{14,12},{16,14},{18,16},{20... | collective-permute-start | bytes 104 | tf_op jit(solution)/shard_map/ppermute | solution.py:27
  135.4 6.1 %collective-permute-start.12 = (f32[8,1]{1,0:T(8,128)S(1)}, f32[8,1]{1,0:T(8,128)S(1)}, u32[]{:S(2)}, u32[]{:S(2)}) collective-permute-start(f32[8,1]{1,0:T(8,128)S(1)} %get-tuple-element.19), channel_id=1, source_target_pairs={{0,2},{2,4},{4,6},{6,8},{8,10},{10,12},{12,14},{14,16},{16,18},{18... | collective-permute-start | bytes 104 | tf_op jit(solution)/shard_map/ppermute | solution.py:26
  142.1 10.8 %collective-permute-start.17 = (f32[8,16384]{1,0:T(8,128)S(1)}, f32[8,16384]{1,0:T(8,128)}, u32[]{:S(2)}, u32[]{:S(2)}) collective-permute-start(f32[8,16384]{1,0:T(8,128)S(1)} %fusion.16), channel_id=1, source_target_pairs={{0,1},{1,0},{2,3},{3,2},{4,5},{5,4},{6,7},{7,6},{8,9},{9,8},{10,11... | collective-permute-start | bytes 1572872 | tf_op jit(solution)/shard_map/ppermute | solution.py:16
  144.8 6.8 %collective-permute-start.16 = (f32[8,1]{1,0:T(8,128)S(1)}, f32[8,1]{1,0:T(8,128)S(1)}, u32[]{:S(2)}, u32[]{:S(2)}) collective-permute-start(f32[8,1]{1,0:T(8,128)S(1)} %get-tuple-element.18), channel_id=1, source_target_pairs={{2,0},{4,2},{6,4},{8,6},{10,8},{12,10},{14,12},{16,14},{18,16},{20... | collective-permute-start | bytes 104 | tf_op jit(solution)/shard_map/ppermute | solution.py:27
  146.1 6.8 %collective-permute-start.15 = (f32[8,1]{1,0:T(8,128)S(1)}, f32[8,1]{1,0:T(8,128)S(1)}, u32[]{:S(2)}, u32[]{:S(2)}) collective-permute-start(f32[8,1]{1,0:T(8,128)S(1)} %get-tuple-element.17), channel_id=1, source_target_pairs={{0,2},{2,4},{4,6},{6,8},{8,10},{10,12},{12,14},{14,16},{16,18},{18... | collective-permute-start | bytes 104 | tf_op jit(solution)/shard_map/ppermute | solution.py:26
  172.0 11.5 %collective-permute-start.20 = (f32[8,16384]{1,0:T(8,128)S(1)}, f32[8,16384]{1,0:T(8,128)S(1)}, u32[]{:S(2)}, u32[]{:S(2)}) collective-permute-start(f32[8,16384]{1,0:T(8,128)S(1)} %fusion.5), channel_id=1, source_target_pairs={{0,1},{1,0},{2,3},{3,2},{4,5},{5,4},{6,7},{7,6},{8,9},{9,8},{10,11... | collective-permute-start | bytes 1572872 | tf_op jit(solution)/shard_map/ppermute | solution.py:16
  174.0 8.2 %collective-permute-start.19 = (f32[8,1]{1,0:T(8,128)S(1)}, f32[8,1]{1,0:T(8,128)S(1)}, u32[]{:S(2)}, u32[]{:S(2)}) collective-permute-start(f32[8,1]{1,0:T(8,128)S(1)} %get-tuple-element.16), channel_id=1, source_target_pairs={{2,0},{4,2},{6,4},{8,6},{10,8},{12,10},{14,12},{16,14},{18,16},{20... | collective-permute-start | bytes 104 | tf_op jit(solution)/shard_map/ppermute | solution.py:27
  175.3 8.3 %collective-permute-start.18 = (f32[8,1]{1,0:T(8,128)S(1)}, f32[8,1]{1,0:T(8,128)S(1)}, u32[]{:S(2)}, u32[]{:S(2)}) collective-permute-start(f32[8,1]{1,0:T(8,128)S(1)} %get-tuple-element.15), channel_id=1, source_target_pairs={{0,2},{2,4},{4,6},{6,8},{8,10},{10,12},{12,14},{14,16},{16,18},{18... | collective-permute-start | bytes 104 | tf_op jit(solution)/shard_map/ppermute | solution.py:26
  184.2 11.5 %collective-permute-start.23 = (f32[8,16384]{1,0:T(8,128)S(1)}, f32[8,16384]{1,0:T(8,128)S(1)}, u32[]{:S(2)}, u32[]{:S(2)}) collective-permute-start(f32[8,16384]{1,0:T(8,128)S(1)} %fusion.50), channel_id=1, source_target_pairs={{0,1},{1,0},{2,3},{3,2},{4,5},{5,4},{6,7},{7,6},{8,9},{9,8},{10,11... | collective-permute-start | bytes 1572872 | tf_op jit(solution)/shard_map/ppermute | solution.py:16
  186.2 8.8 %collective-permute-start.22 = (f32[8,1]{1,0:T(8,128)S(1)}, f32[8,1]{1,0:T(8,128)S(1)}, u32[]{:S(2)}, u32[]{:S(2)}) collective-permute-start(f32[8,1]{1,0:T(8,128)S(1)} %get-tuple-element.14), channel_id=1, source_target_pairs={{2,0},{4,2},{6,4},{8,6},{10,8},{12,10},{14,12},{16,14},{18,16},{20... | collective-permute-start | bytes 104 | tf_op jit(solution)/shard_map/ppermute | solution.py:27
  187.5 8.2 %collective-permute-start.21 = (f32[8,1]{1,0:T(8,128)S(1)}, f32[8,1]{1,0:T(8,128)S(1)}, u32[]{:S(2)}, u32[]{:S(2)}) collective-permute-start(f32[8,1]{1,0:T(8,128)S(1)} %get-tuple-element.13), channel_id=1, source_target_pairs={{0,2},{2,4},{4,6},{6,8},{8,10},{10,12},{12,14},{14,16},{16,18},{18... | collective-permute-start | bytes 104 | tf_op jit(solution)/shard_map/ppermute | solution.py:26
  196.2 11.5 %collective-permute-start.26 = (f32[8,16384]{1,0:T(8,128)S(1)}, f32[8,16384]{1,0:T(8,128)S(1)}, u32[]{:S(2)}, u32[]{:S(2)}) collective-permute-start(f32[8,16384]{1,0:T(8,128)S(1)} %fusion.44), channel_id=1, source_target_pairs={{0,1},{1,0},{2,3},{3,2},{4,5},{5,4},{6,7},{7,6},{8,9},{9,8},{10,11... | collective-permute-start | bytes 1572872 | tf_op jit(solution)/shard_map/ppermute | solution.py:16
  198.2 8.2 %collective-permute-start.25 = (f32[8,1]{1,0:T(8,128)S(1)}, f32[8,1]{1,0:T(8,128)S(1)}, u32[]{:S(2)}, u32[]{:S(2)}) collective-permute-start(f32[8,1]{1,0:T(8,128)S(1)} %get-tuple-element.12), channel_id=1, source_target_pairs={{2,0},{4,2},{6,4},{8,6},{10,8},{12,10},{14,12},{16,14},{18,16},{20... | collective-permute-start | bytes 104 | tf_op jit(solution)/shard_map/ppermute | solution.py:27
  199.5 8.2 %collective-permute-start.24 = (f32[8,1]{1,0:T(8,128)S(1)}, f32[8,1]{1,0:T(8,128)S(1)}, u32[]{:S(2)}, u32[]{:S(2)}) collective-permute-start(f32[8,1]{1,0:T(8,128)S(1)} %get-tuple-element.11), channel_id=1, source_target_pairs={{0,2},{2,4},{4,6},{6,8},{8,10},{10,12},{12,14},{14,16},{16,18},{18... | collective-permute-start | bytes 104 | tf_op jit(solution)/shard_map/ppermute | solution.py:26
  208.4 14.0 %collective-permute-start.29 = (f32[8,16384]{1,0:T(8,128)S(1)}, f32[8,16384]{1,0:T(8,128)S(1)}, u32[]{:S(2)}, u32[]{:S(2)}) collective-permute-start(f32[8,16384]{1,0:T(8,128)S(1)} %fusion.38), channel_id=1, source_target_pairs={{0,1},{1,0},{2,3},{3,2},{4,5},{5,4},{6,7},{7,6},{8,9},{9,8},{10,11... | collective-permute-start | bytes 1572872 | tf_op jit(solution)/shard_map/ppermute | solution.py:16
  210.3 23.2 %collective-permute-start.33 = (f32[8,16384]{1,0:T(8,128)S(1)}, f32[8,16384]{1,0:T(8,128)S(1)}, u32[]{:S(2)}, u32[]{:S(2)}) collective-permute-start(f32[8,16384]{1,0:T(8,128)S(1)} %fusion.18), channel_id=1, source_target_pairs={{0,1},{1,0},{2,3},{3,2},{4,5},{5,4},{6,7},{7,6},{8,9},{9,8},{10,11... | collective-permute-start | bytes 1572872 | tf_op jit(solution)/shard_map/ppermute | solution.py:16
  212.8 8.8 %collective-permute-start.28 = (f32[8,1]{1,0:T(8,128)S(1)}, f32[8,1]{1,0:T(8,128)S(1)}, u32[]{:S(2)}, u32[]{:S(2)}) collective-permute-start(f32[8,1]{1,0:T(8,128)S(1)} %get-tuple-element.10), channel_id=1, source_target_pairs={{2,0},{4,2},{6,4},{8,6},{10,8},{12,10},{14,12},{16,14},{18,16},{20... | collective-permute-start | bytes 104 | tf_op jit(solution)/shard_map/ppermute | solution.py:27
  214.1 8.3 %collective-permute-start.27 = (f32[8,1]{1,0:T(8,128)S(1)}, f32[8,1]{1,0:T(8,128)S(1)}, u32[]{:S(2)}, u32[]{:S(2)}) collective-permute-start(f32[8,1]{1,0:T(8,128)S(1)} %get-tuple-element.9), channel_id=1, source_target_pairs={{0,2},{2,4},{4,6},{6,8},{8,10},{10,12},{12,14},{14,16},{16,18},{18... | collective-permute-start | bytes 104 | tf_op jit(solution)/shard_map/ppermute | solution.py:26
  222.8 11.5 %collective-permute-start.32 = (f32[8,16384]{1,0:T(8,128)S(1)}, f32[8,16384]{1,0:T(8,128)S(1)}, u32[]{:S(2)}, u32[]{:S(2)}) collective-permute-start(f32[8,16384]{1,0:T(8,128)S(1)} %fusion.32), channel_id=1, source_target_pairs={{0,1},{1,0},{2,3},{3,2},{4,5},{5,4},{6,7},{7,6},{8,9},{9,8},{10,11... | collective-permute-start | bytes 1572872 | tf_op jit(solution)/shard_map/ppermute | solution.py:16
  224.8 8.8 %collective-permute-start.31 = (f32[8,1]{1,0:T(8,128)S(1)}, f32[8,1]{1,0:T(8,128)S(1)}, u32[]{:S(2)}, u32[]{:S(2)}) collective-permute-start(f32[8,1]{1,0:T(8,128)S(1)} %get-tuple-element.8), channel_id=1, source_target_pairs={{2,0},{4,2},{6,4},{8,6},{10,8},{12,10},{14,12},{16,14},{18,16},{20... | collective-permute-start | bytes 104 | tf_op jit(solution)/shard_map/ppermute | solution.py:27
  226.1 8.2 %collective-permute-start.30 = (f32[8,1]{1,0:T(8,128)S(1)}, f32[8,1]{1,0:T(8,128)S(1)}, u32[]{:S(2)}, u32[]{:S(2)}) collective-permute-start(f32[8,1]{1,0:T(8,128)S(1)} %get-tuple-element.7), channel_id=1, source_target_pairs={{0,2},{2,4},{4,6},{6,8},{8,10},{10,12},{12,14},{14,16},{16,18},{18... | collective-permute-start | bytes 104 | tf_op jit(solution)/shard_map/ppermute | solution.py:26
Sparse Core Ops, SparseCore 0:
  10.5 86.5 all-gather.1
  237.0 242.0 reduce-scatter.1
where the time goes:
time: 534 us; the launch traced here: 533 us
  waiting for transfers between devices  332 us (62%)
  starting transfers between devices  101 us (19%)
  blocking collectives  46.9 us (9%)
  local copies, waits for them, and re-layouts  14.9 us (3%)
  between operations  14 us (3%)
  other arithmetic  13.9 us (3%)
  matrix products  10.1 us (2%)
    reduce_scatter x1, waiting for transfers between devices, local(): lax.psum_scatter(jnp.zeros((inv_rows * lax.axis_size('mesh'), CELLS), jnp...  242 us
    all_gather x1, waiting for transfers between devices, local(): gathered = lax.all_gather(log_sigma, 'mesh', axis=0, tiled=True)  78.7 us
    ppermute x11, starting transfers between devices, with_halo(): before = lax.ppermute(last, axis, up)  63.6 us
    psum x1, blocking collectives, local(): return lax.psum(owned, ('group', 'comp'))  46.9 us
    ppermute x12, starting transfers between devices, from_partner(): return lax.ppermute(value, axis, pairs)  23.5 us
    ppermute x11, starting transfers between devices, with_halo(): after = lax.ppermute(initial, axis, down)  14.1 us
  transfers between devices with their start and end apart: 36, of which 12 were waited for; matrix products, arithmetic and copies ran while one was open for 2% of the time, Pallas kernels for 0%

commit v1 on v0

--- a/solution.py
+++ b/solution.py
@@ -88,7 +88,7 @@
         scatter_dimension=0,
         tiled=True,
     )
-    return lax.psum(owned, ("group", "comp"))
+    return lax.psum(lax.psum(owned, "group"), "comp")
 
 
 def solution(mesh):

time: 534 us -> 523 us (0.979)
  the two profiles are of different devices: /device:TPU:32 before, /device:TPU:1 now
where the time goes in v1:
time: 523 us; the launch traced here: 522 us
  waiting for transfers between devices  311 us (59%)
  starting transfers between devices  118 us (23%)
  blocking collectives  40.1 us (8%)
  local copies, waits for them, and re-layouts  14.8 us (3%)
  between operations  14 us (3%)
  other arithmetic  13.8 us (3%)
  matrix products  10.1 us (2%)
    reduce_scatter x1, waiting for transfers between devices, local(): lax.psum_scatter(jnp.zeros((inv_rows * lax.axis_size('mesh'), CELLS), jnp...  237 us
    all_gather x1, waiting for transfers between devices, local(): gathered = lax.all_gather(log_sigma, 'mesh', axis=0, tiled=True)  68.6 us
    ppermute x11, starting transfers between devices, with_halo(): before = lax.ppermute(last, axis, up)  60.5 us
    ppermute x12, starting transfers between devices, from_partner(): return lax.ppermute(value, axis, pairs)  43.4 us
    psum x2, blocking collectives, local(): return lax.psum(lax.psum(owned, 'group'), 'comp')  40.1 us
    ppermute x11, starting transfers between devices, with_halo(): after = lax.ppermute(initial, axis, down)  14.1 us
  transfers between devices with their start and end apart: 36, of which 12 were waited for; matrix products, arithmetic and copies ran while one was open for 2% of the time, Pallas kernels for 0%

profile of v1, /device:TPU:1, one launch (start us, length us, event | category | flops | bytes accessed | tf_op | source)
XLA Modules:
  0.0 522.0 jit_solution(16118567560543336165)
XLA Ops:
  6.5 0.7 all-gather.2.cloned.1.call-update
  7.3 1.3 collective-permute-start.1
  8.6 4.6 collective-permute-start
  13.3 8.8 %collective-permute-start.2 = (f32[8,16384]{1,0:T(8,128)S(1)}, f32[8,16384]{1,0:T(8,128)S(1)}, u32[]{:S(2)}, u32[]{:S(2)}) collective-permute-start(f32[8,16384]{1,0:T(8,128)S(1)} %broadcast.154.clone), channel_id=1, source_target_pairs={{0,1},{1,0},{2,3},{3,2},{4,5},{5,4},{6,7},{7,6},{8,9},{9,8},{10,11... | collective-permute-start | bytes 1572872 | tf_op jit(solution)/shard_map/ppermute | solution.py:16
  22.1 1.2 gather_fusion.1
  23.3 0.6 convolution_bitcast_fusion.11
  23.9 0.7 compare_and_fusion
  24.6 0.7 fusion.121
  25.3 68.6 %all-gather.2.cloned.1.call-done = f32[2048,128]{1,0:T(8,128)} async-done(((f32[64,128]{1,0:T(8,128)}), f32[2048,128]{1,0:T(8,128)}) %all-gather.2.cloned.1.call-update) | async-done | bytes 1048592 | tf_op jit(solution)/shard_map/all_gather | solution.py:66
  93.9 1.9 gather_fusion
  95.9 1.7 fusion.8
  97.5 7.0 %collective-permute-start.5 = (f32[8,16384]{1,0:T(8,128)S(1)}, f32[8,16384]{1,0:T(8,128)S(1)}, u32[]{:S(2)}, u32[]{:S(2)}) collective-permute-start(f32[8,16384]{1,0:T(8,128)S(1)} %fusion.8), channel_id=1, source_target_pairs={{0,1},{1,0},{2,3},{3,2},{4,5},{5,4},{6,7},{7,6},{8,9},{9,8},{10,11... | collective-permute-start | bytes 1572872 | tf_op jit(solution)/shard_map/ppermute | solution.py:16
  104.6 1.3 collective-permute-start.4
  105.9 4.0 collective-permute-start.3
  109.9 0.7 collective-permute-done.3
  110.7 1.9 fusion.10
  112.6 3.1 collective-permute-start.8
  115.7 1.3 collective-permute-start.7
  117.0 4.5 collective-permute-start.6
  121.6 0.6 convolution_bitcast_fusion.8
  122.8 2.8 collective-permute-start.11
  125.7 1.3 collective-permute-start.10
  126.9 4.5 collective-permute-start.9
  131.5 0.7 collective-permute-done.9
  132.2 0.9 fusion.14
  133.1 2.8 collective-permute-start.14
  136.0 1.3 collective-permute-start.13
  137.3 4.5 collective-permute-start.12
  141.8 0.6 convolution_bitcast_fusion.6
  143.1 2.8 collective-permute-start.17
  146.6 1.3 collective-permute-start.16
  147.9 5.2 collective-permute-start.15
  153.1 0.7 collective-permute-done.15
  153.9 1.9 fusion.18
  155.8 5.3 %copy.271 = f32[8,16384]{0,1:T(8,128)} copy(f32[8,16384]{1,0:T(8,128)S(1)} %fusion.18) | data formatting | bytes 1048576 | tf_op jit(solution)/shard_map/add | solution.py:56
  161.1 6.0 %scatter_custom_fusion = f32[8,16384]{0,1:T(8,128)} fusion(s32[128]{0:T(128)S(1)} %fusion.122, f32[]{:T(128)} %constant.12.clone.1, f32[1,1,8,128]{2,3,1,0:T(8,128)S(1)} %copy.272, f32[8,16384]{0,1:T(8,128)} %copy.271, s32[1024]{0:T(1024)S(1)} %pad_clamp_fusion), kind=kCustom, calls=%fused_computation.15 | custom fusion | flops 2048 | bytes 1118212 | tf_op jit(solution)/shard_map/scatter-add | solution.py:77
  167.0 5.5 %copy.273 = f32[8,16384]{1,0:T(8,128)S(1)} copy(f32[8,16384]{0,1:T(8,128)} %scatter_custom_fusion) | data formatting | bytes 1048576 | tf_op jit(solution)/shard_map/scatter-add | solution.py:77
  173.0 2.8 collective-permute-start.20
  175.9 1.3 collective-permute-start.19
  177.2 6.6 %collective-permute-start.18 = (f32[8,1]{1,0:T(8,128)S(1)}, f32[8,1]{1,0:T(8,128)S(1)}, u32[]{:S(2)}, u32[]{:S(2)}) collective-permute-start(f32[8,1]{1,0:T(8,128)S(1)} %get-tuple-element.15), channel_id=1, source_target_pairs={{0,2},{2,4},{4,6},{6,8},{8,10},{10,12},{12,14},{14,16},{16,18},{18... | collective-permute-start | bytes 104 | tf_op jit(solution)/shard_map/ppermute | solution.py:26
  183.8 0.7 collective-permute-done.18
  184.5 0.7 fusion.50
  185.2 2.8 collective-permute-start.23
  188.1 1.3 collective-permute-start.22
  189.4 6.6 %collective-permute-start.21 = (f32[8,1]{1,0:T(8,128)S(1)}, f32[8,1]{1,0:T(8,128)S(1)}, u32[]{:S(2)}, u32[]{:S(2)}) collective-permute-start(f32[8,1]{1,0:T(8,128)S(1)} %get-tuple-element.13), channel_id=1, source_target_pairs={{0,2},{2,4},{4,6},{6,8},{8,10},{10,12},{12,14},{14,16},{16,18},{18... | collective-permute-start | bytes 104 | tf_op jit(solution)/shard_map/ppermute | solution.py:26
  196.0 0.6 convolution_bitcast_fusion.3
  197.2 2.8 collective-permute-start.26
  200.0 1.3 collective-permute-start.25
  201.3 6.7 %collective-permute-start.24 = (f32[8,1]{1,0:T(8,128)S(1)}, f32[8,1]{1,0:T(8,128)S(1)}, u32[]{:S(2)}, u32[]{:S(2)}) collective-permute-start(f32[8,1]{1,0:T(8,128)S(1)} %get-tuple-element.11), channel_id=1, source_target_pairs={{0,2},{2,4},{4,6},{6,8},{8,10},{10,12},{12,14},{14,16},{16,18},{18... | collective-permute-start | bytes 104 | tf_op jit(solution)/shard_map/ppermute | solution.py:26
  208.0 0.7 collective-permute-done.24
  208.7 0.7 fusion.38
  209.4 2.8 collective-permute-start.29
  212.2 1.9 collective-permute-start.33
  214.2 1.3 collective-permute-start.28
  215.5 6.6 %collective-permute-start.27 = (f32[8,1]{1,0:T(8,128)S(1)}, f32[8,1]{1,0:T(8,128)S(1)}, u32[]{:S(2)}, u32[]{:S(2)}) collective-permute-start(f32[8,1]{1,0:T(8,128)S(1)} %get-tuple-element.9), channel_id=1, source_target_pairs={{0,2},{2,4},{4,6},{6,8},{8,10},{10,12},{12,14},{14,16},{16,18},{18... | collective-permute-start | bytes 104 | tf_op jit(solution)/shard_map/ppermute | solution.py:26
  222.1 0.6 convolution_bitcast_fusion.1
  223.3 3.3 collective-permute-start.32
  226.6 1.3 collective-permute-start.31
  227.9 6.6 %collective-permute-start.30 = (f32[8,1]{1,0:T(8,128)S(1)}, f32[8,1]{1,0:T(8,128)S(1)}, u32[]{:S(2)}, u32[]{:S(2)}) collective-permute-start(f32[8,1]{1,0:T(8,128)S(1)} %get-tuple-element.7), channel_id=1, source_target_pairs={{0,2},{2,4},{4,6},{6,8},{8,10},{10,12},{12,14},{14,16},{16,18},{18... | collective-permute-start | bytes 104 | tf_op jit(solution)/shard_map/ppermute | solution.py:26
  234.5 0.6 convolution_bitcast_fusion
  235.7 2.1 scatter_custom_fusion.1
  237.8 237.3 %reduce-scatter.2.cloned.1.call-done = f32[64,128]{1,0:T(8,128)} async-done(((f32[2048,128]{1,0:T(8,128)}), f32[64,128]{1,0:T(8,128)}) %reduce-scatter.2.cloned.1.call-update) | async-done | bytes 32784 | tf_op jit(solution)/shard_map/reduce_scatter | solution.py:83
  475.1 23.2 %psum.14 = f32[64,128]{1,0:T(8,128)S(1)} all-reduce(f32[64,128]{1,0:T(8,128)} %reduce-scatter.2.cloned.1.call-done), channel_id=1, replica_groups=mesh['group'=8,'mesh'=32,'comp'=2] {'group'}, use_global_device_ids=true, to_apply=%region_4.5 | all-reduce | flops 8192 | bytes 65536 | tf_op jit(solution)/shard_map/psum | solution.py:91
  498.2 16.9 %psum.15 = f32[64,128]{1,0:T(8,128)} all-reduce(f32[64,128]{1,0:T(8,128)S(1)} %psum.14), channel_id=1, replica_groups=mesh['group'=8,'mesh'=32,'comp'=2] {'comp'}, use_global_device_ids=true, to_apply=%region_5.6 | all-reduce | flops 8192 | bytes 65536 | tf_op jit(solution)/shard_map/psum | solution.py:91
  (67 shorter events, 5.1 us)
Async XLA Ops:
  6.5 15.5 %copy-start = (f32[128,128]{1,0:T(8,128)S(1)}, f32[128,128]{1,0:T(8,128)}, u32[]{:S(2)}) copy-start(f32[128,128]{1,0:T(8,128)} %param.10) | copy-start | bytes 196612
  6.5 115.8 %copy-start.1 = (f32[1,1,8,128,128]{4,3,2,1,0:T(8,128)S(1)}, f32[1,1,8,128,128]{4,3,2,1,0:T(8,128)}, u32[]{:S(2)}) copy-start(f32[1,1,8,128,128]{4,3,2,1,0:T(8,128)} %param.11) | copy-start | bytes 1572868
  6.5 87.3 %all-gather.2.cloned.1.call-start = ((), (), s32[]{:S(2)}) async-start(), calls=%async_computation.1 | async-start | bytes 1081344 | tf_op jit(solution)/shard_map/all_gather | solution.py:66
  7.3 467.8 %reduce-scatter.2.cloned.1.call-start = ((), (), s32[]{:S(2)}) async-start(), calls=%async_computation.2 | async-start | bytes 1081344 | tf_op jit(solution)/shard_map/reduce_scatter | solution.py:83
  7.3 88.5 %collective-permute-start.1 = (f32[8,1]{1,0:T(8,128)S(1)}, f32[8,1]{1,0:T(8,128)S(1)}, u32[]{:S(2)}, u32[]{:S(2)}) collective-permute-start(f32[8,1]{1,0:T(8,128)S(1)} %broadcast.157), channel_id=1, source_target_pairs={{2,0},{4,2},{6,4},{8,6},{10,8},{12,10},{14,12},{16,14},{18,16},{20... | collective-permute-start | bytes 104 | tf_op jit(solution)/shard_map/ppermute | solution.py:27
  8.6 87.2 %collective-permute-start = (f32[8,1]{1,0:T(8,128)S(1)}, f32[8,1]{1,0:T(8,128)S(1)}, u32[]{:S(2)}, u32[]{:S(2)}) collective-permute-start(f32[8,1]{1,0:T(8,128)S(1)} %broadcast.157), channel_id=1, source_target_pairs={{0,2},{2,4},{4,6},{6,8},{8,10},{10,12},{12,14},{14,16},{16,18},{18... | collective-permute-start | bytes 104 | tf_op jit(solution)/shard_map/ppermute | solution.py:26
  13.2 132.6 %copy-start.3 = (s32[1,128]{1,0:T(1,128)S(1)}, s32[1,128]{1,0:T(1,128)}, u32[]{:S(2)}) copy-start(s32[1,128]{1,0:T(1,128)} %param.12) | copy-start | bytes 1540
  13.3 132.6 %copy-start.2 = (f32[1,1,8,128]{3,2,1,0:T(8,128)S(1)}, f32[1,1,8,128]{3,2,1,0:T(8,128)}, u32[]{:S(2)}) copy-start(f32[1,1,8,128]{3,2,1,0:T(8,128)} %param.13) | copy-start | bytes 12292
  13.3 82.6 %collective-permute-start.2 = (f32[8,16384]{1,0:T(8,128)S(1)}, f32[8,16384]{1,0:T(8,128)S(1)}, u32[]{:S(2)}, u32[]{:S(2)}) collective-permute-start(f32[8,16384]{1,0:T(8,128)S(1)} %broadcast.154.clone), channel_id=1, source_target_pairs={{0,1},{1,0},{2,3},{3,2},{4,5},{5,4},{6,7},{7,6},{8,9},{9,8},{10,11... | collective-permute-start | bytes 1572872 | tf_op jit(solution)/shard_map/ppermute | solution.py:16
  97.5 13.1 %collective-permute-start.5 = (f32[8,16384]{1,0:T(8,128)S(1)}, f32[8,16384]{1,0:T(8,128)S(1)}, u32[]{:S(2)}, u32[]{:S(2)}) collective-permute-start(f32[8,16384]{1,0:T(8,128)S(1)} %fusion.8), channel_id=1, source_target_pairs={{0,1},{1,0},{2,3},{3,2},{4,5},{5,4},{6,7},{7,6},{8,9},{9,8},{10,11... | collective-permute-start | bytes 1572872 | tf_op jit(solution)/shard_map/ppermute | solution.py:16
  104.6 5.3 %collective-permute-start.4 = (f32[8,1]{1,0:T(8,128)S(1)}, f32[8,1]{1,0:T(8,128)S(1)}, u32[]{:S(2)}, u32[]{:S(2)}) collective-permute-start(f32[8,1]{1,0:T(8,128)S(1)} %get-tuple-element.26), channel_id=1, source_target_pairs={{2,0},{4,2},{6,4},{8,6},{10,8},{12,10},{14,12},{16,14},{18,16},{20... | collective-permute-start | bytes 104 | tf_op jit(solution)/shard_map/ppermute | solution.py:27
  105.9 4.7 collective-permute-start.3
  112.6 9.7 %collective-permute-start.8 = (f32[8,16384]{1,0:T(8,128)S(1)}, f32[8,16384]{1,0:T(8,128)S(1)}, u32[]{:S(2)}, u32[]{:S(2)}) collective-permute-start(f32[8,16384]{1,0:T(8,128)S(1)} %fusion.10), channel_id=1, source_target_pairs={{0,1},{1,0},{2,3},{3,2},{4,5},{5,4},{6,7},{7,6},{8,9},{9,8},{10,11... | collective-permute-start | bytes 1572872 | tf_op jit(solution)/shard_map/ppermute | solution.py:16
  115.7 6.4 %collective-permute-start.7 = (f32[8,1]{1,0:T(8,128)S(1)}, f32[8,1]{1,0:T(8,128)S(1)}, u32[]{:S(2)}, u32[]{:S(2)}) collective-permute-start(f32[8,1]{1,0:T(8,128)S(1)} %get-tuple-element.24), channel_id=1, source_target_pairs={{2,0},{4,2},{6,4},{8,6},{10,8},{12,10},{14,12},{16,14},{18,16},{20... | collective-permute-start | bytes 104 | tf_op jit(solution)/shard_map/ppermute | solution.py:27
  117.0 5.3 %collective-permute-start.6 = (f32[8,1]{1,0:T(8,128)S(1)}, f32[8,1]{1,0:T(8,128)S(1)}, u32[]{:S(2)}, u32[]{:S(2)}) collective-permute-start(f32[8,1]{1,0:T(8,128)S(1)} %get-tuple-element.23), channel_id=1, source_target_pairs={{0,2},{2,4},{4,6},{6,8},{8,10},{10,12},{12,14},{14,16},{16,18},{18... | collective-permute-start | bytes 104 | tf_op jit(solution)/shard_map/ppermute | solution.py:26
  122.8 9.4 %collective-permute-start.11 = (f32[8,16384]{1,0:T(8,128)S(1)}, f32[8,16384]{1,0:T(8,128)S(1)}, u32[]{:S(2)}, u32[]{:S(2)}) collective-permute-start(f32[8,16384]{1,0:T(8,128)S(1)} %fusion.12), channel_id=1, source_target_pairs={{0,1},{1,0},{2,3},{3,2},{4,5},{5,4},{6,7},{7,6},{8,9},{9,8},{10,11... | collective-permute-start | bytes 1572872 | tf_op jit(solution)/shard_map/ppermute | solution.py:16
  125.7 5.8 %collective-permute-start.10 = (f32[8,1]{1,0:T(8,128)S(1)}, f32[8,1]{1,0:T(8,128)S(1)}, u32[]{:S(2)}, u32[]{:S(2)}) collective-permute-start(f32[8,1]{1,0:T(8,128)S(1)} %get-tuple-element.22), channel_id=1, source_target_pairs={{2,0},{4,2},{6,4},{8,6},{10,8},{12,10},{14,12},{16,14},{18,16},{20... | collective-permute-start | bytes 104 | tf_op jit(solution)/shard_map/ppermute | solution.py:27
  126.9 5.3 %collective-permute-start.9 = (f32[8,1]{1,0:T(8,128)S(1)}, f32[8,1]{1,0:T(8,128)S(1)}, u32[]{:S(2)}, u32[]{:S(2)}) collective-permute-start(f32[8,1]{1,0:T(8,128)S(1)} %get-tuple-element.21), channel_id=1, source_target_pairs={{0,2},{2,4},{4,6},{6,8},{8,10},{10,12},{12,14},{14,16},{16,18},{18... | collective-permute-start | bytes 104 | tf_op jit(solution)/shard_map/ppermute | solution.py:26
  133.1 9.4 %collective-permute-start.14 = (f32[8,16384]{1,0:T(8,128)S(1)}, f32[8,16384]{1,0:T(8,128)S(1)}, u32[]{:S(2)}, u32[]{:S(2)}) collective-permute-start(f32[8,16384]{1,0:T(8,128)S(1)} %fusion.14), channel_id=1, source_target_pairs={{0,1},{1,0},{2,3},{3,2},{4,5},{5,4},{6,7},{7,6},{8,9},{9,8},{10,11... | collective-permute-start | bytes 1572872 | tf_op jit(solution)/shard_map/ppermute | solution.py:16
  136.0 6.4 %collective-permute-start.13 = (f32[8,1]{1,0:T(8,128)S(1)}, f32[8,1]{1,0:T(8,128)S(1)}, u32[]{:S(2)}, u32[]{:S(2)}) collective-permute-start(f32[8,1]{1,0:T(8,128)S(1)} %get-tuple-element.20), channel_id=1, source_target_pairs={{2,0},{4,2},{6,4},{8,6},{10,8},{12,10},{14,12},{16,14},{18,16},{20... | collective-permute-start | bytes 104 | tf_op jit(solution)/shard_map/ppermute | solution.py:27
  137.3 5.3 %collective-permute-start.12 = (f32[8,1]{1,0:T(8,128)S(1)}, f32[8,1]{1,0:T(8,128)S(1)}, u32[]{:S(2)}, u32[]{:S(2)}) collective-permute-start(f32[8,1]{1,0:T(8,128)S(1)} %get-tuple-element.19), channel_id=1, source_target_pairs={{0,2},{2,4},{4,6},{6,8},{8,10},{10,12},{12,14},{14,16},{16,18},{18... | collective-permute-start | bytes 104 | tf_op jit(solution)/shard_map/ppermute | solution.py:26
  143.1 10.8 %collective-permute-start.17 = (f32[8,16384]{1,0:T(8,128)S(1)}, f32[8,16384]{1,0:T(8,128)}, u32[]{:S(2)}, u32[]{:S(2)}) collective-permute-start(f32[8,16384]{1,0:T(8,128)S(1)} %fusion.16), channel_id=1, source_target_pairs={{0,1},{1,0},{2,3},{3,2},{4,5},{5,4},{6,7},{7,6},{8,9},{9,8},{10,11... | collective-permute-start | bytes 1572872 | tf_op jit(solution)/shard_map/ppermute | solution.py:16
  146.6 6.5 %collective-permute-start.16 = (f32[8,1]{1,0:T(8,128)S(1)}, f32[8,1]{1,0:T(8,128)S(1)}, u32[]{:S(2)}, u32[]{:S(2)}) collective-permute-start(f32[8,1]{1,0:T(8,128)S(1)} %get-tuple-element.18), channel_id=1, source_target_pairs={{2,0},{4,2},{6,4},{8,6},{10,8},{12,10},{14,12},{16,14},{18,16},{20... | collective-permute-start | bytes 104 | tf_op jit(solution)/shard_map/ppermute | solution.py:27
  147.9 5.9 %collective-permute-start.15 = (f32[8,1]{1,0:T(8,128)S(1)}, f32[8,1]{1,0:T(8,128)S(1)}, u32[]{:S(2)}, u32[]{:S(2)}) collective-permute-start(f32[8,1]{1,0:T(8,128)S(1)} %get-tuple-element.17), channel_id=1, source_target_pairs={{0,2},{2,4},{4,6},{6,8},{8,10},{10,12},{12,14},{14,16},{16,18},{18... | collective-permute-start | bytes 104 | tf_op jit(solution)/shard_map/ppermute | solution.py:26
  173.0 11.5 %collective-permute-start.20 = (f32[8,16384]{1,0:T(8,128)S(1)}, f32[8,16384]{1,0:T(8,128)S(1)}, u32[]{:S(2)}, u32[]{:S(2)}) collective-permute-start(f32[8,16384]{1,0:T(8,128)S(1)} %fusion.5), channel_id=1, source_target_pairs={{0,1},{1,0},{2,3},{3,2},{4,5},{5,4},{6,7},{7,6},{8,9},{9,8},{10,11... | collective-permute-start | bytes 1572872 | tf_op jit(solution)/shard_map/ppermute | solution.py:16
  175.9 7.9 %collective-permute-start.19 = (f32[8,1]{1,0:T(8,128)S(1)}, f32[8,1]{1,0:T(8,128)S(1)}, u32[]{:S(2)}, u32[]{:S(2)}) collective-permute-start(f32[8,1]{1,0:T(8,128)S(1)} %get-tuple-element.16), channel_id=1, source_target_pairs={{2,0},{4,2},{6,4},{8,6},{10,8},{12,10},{14,12},{16,14},{18,16},{20... | collective-permute-start | bytes 104 | tf_op jit(solution)/shard_map/ppermute | solution.py:27
  177.2 7.4 %collective-permute-start.18 = (f32[8,1]{1,0:T(8,128)S(1)}, f32[8,1]{1,0:T(8,128)S(1)}, u32[]{:S(2)}, u32[]{:S(2)}) collective-permute-start(f32[8,1]{1,0:T(8,128)S(1)} %get-tuple-element.15), channel_id=1, source_target_pairs={{0,2},{2,4},{4,6},{6,8},{8,10},{10,12},{12,14},{14,16},{16,18},{18... | collective-permute-start | bytes 104 | tf_op jit(solution)/shard_map/ppermute | solution.py:26
  185.2 11.5 %collective-permute-start.23 = (f32[8,16384]{1,0:T(8,128)S(1)}, f32[8,16384]{1,0:T(8,128)S(1)}, u32[]{:S(2)}, u32[]{:S(2)}) collective-permute-start(f32[8,16384]{1,0:T(8,128)S(1)} %fusion.50), channel_id=1, source_target_pairs={{0,1},{1,0},{2,3},{3,2},{4,5},{5,4},{6,7},{7,6},{8,9},{9,8},{10,11... | collective-permute-start | bytes 1572872 | tf_op jit(solution)/shard_map/ppermute | solution.py:16
  188.1 8.5 %collective-permute-start.22 = (f32[8,1]{1,0:T(8,128)S(1)}, f32[8,1]{1,0:T(8,128)S(1)}, u32[]{:S(2)}, u32[]{:S(2)}) collective-permute-start(f32[8,1]{1,0:T(8,128)S(1)} %get-tuple-element.14), channel_id=1, source_target_pairs={{2,0},{4,2},{6,4},{8,6},{10,8},{12,10},{14,12},{16,14},{18,16},{20... | collective-permute-start | bytes 104 | tf_op jit(solution)/shard_map/ppermute | solution.py:27
  189.4 7.4 %collective-permute-start.21 = (f32[8,1]{1,0:T(8,128)S(1)}, f32[8,1]{1,0:T(8,128)S(1)}, u32[]{:S(2)}, u32[]{:S(2)}) collective-permute-start(f32[8,1]{1,0:T(8,128)S(1)} %get-tuple-element.13), channel_id=1, source_target_pairs={{0,2},{2,4},{4,6},{6,8},{8,10},{10,12},{12,14},{14,16},{16,18},{18... | collective-permute-start | bytes 104 | tf_op jit(solution)/shard_map/ppermute | solution.py:26
  197.2 11.5 %collective-permute-start.26 = (f32[8,16384]{1,0:T(8,128)S(1)}, f32[8,16384]{1,0:T(8,128)S(1)}, u32[]{:S(2)}, u32[]{:S(2)}) collective-permute-start(f32[8,16384]{1,0:T(8,128)S(1)} %fusion.44), channel_id=1, source_target_pairs={{0,1},{1,0},{2,3},{3,2},{4,5},{5,4},{6,7},{7,6},{8,9},{9,8},{10,11... | collective-permute-start | bytes 1572872 | tf_op jit(solution)/shard_map/ppermute | solution.py:16
  200.0 8.0 %collective-permute-start.25 = (f32[8,1]{1,0:T(8,128)S(1)}, f32[8,1]{1,0:T(8,128)S(1)}, u32[]{:S(2)}, u32[]{:S(2)}) collective-permute-start(f32[8,1]{1,0:T(8,128)S(1)} %get-tuple-element.12), channel_id=1, source_target_pairs={{2,0},{4,2},{6,4},{8,6},{10,8},{12,10},{14,12},{16,14},{18,16},{20... | collective-permute-start | bytes 104 | tf_op jit(solution)/shard_map/ppermute | solution.py:27
  201.3 7.4 %collective-permute-start.24 = (f32[8,1]{1,0:T(8,128)S(1)}, f32[8,1]{1,0:T(8,128)S(1)}, u32[]{:S(2)}, u32[]{:S(2)}) collective-permute-start(f32[8,1]{1,0:T(8,128)S(1)} %get-tuple-element.11), channel_id=1, source_target_pairs={{0,2},{2,4},{4,6},{6,8},{8,10},{10,12},{12,14},{14,16},{16,18},{18... | collective-permute-start | bytes 104 | tf_op jit(solution)/shard_map/ppermute | solution.py:26
  209.4 13.4 %collective-permute-start.29 = (f32[8,16384]{1,0:T(8,128)S(1)}, f32[8,16384]{1,0:T(8,128)S(1)}, u32[]{:S(2)}, u32[]{:S(2)}) collective-permute-start(f32[8,16384]{1,0:T(8,128)S(1)} %fusion.38), channel_id=1, source_target_pairs={{0,1},{1,0},{2,3},{3,2},{4,5},{5,4},{6,7},{7,6},{8,9},{9,8},{10,11... | collective-permute-start | bytes 1572872 | tf_op jit(solution)/shard_map/ppermute | solution.py:16
  212.2 22.9 %collective-permute-start.33 = (f32[8,16384]{1,0:T(8,128)S(1)}, f32[8,16384]{1,0:T(8,128)S(1)}, u32[]{:S(2)}, u32[]{:S(2)}) collective-permute-start(f32[8,16384]{1,0:T(8,128)S(1)} %fusion.18), channel_id=1, source_target_pairs={{0,1},{1,0},{2,3},{3,2},{4,5},{5,4},{6,7},{7,6},{8,9},{9,8},{10,11... | collective-permute-start | bytes 1572872 | tf_op jit(solution)/shard_map/ppermute | solution.py:16
  214.2 8.5 %collective-permute-start.28 = (f32[8,1]{1,0:T(8,128)S(1)}, f32[8,1]{1,0:T(8,128)S(1)}, u32[]{:S(2)}, u32[]{:S(2)}) collective-permute-start(f32[8,1]{1,0:T(8,128)S(1)} %get-tuple-element.10), channel_id=1, source_target_pairs={{2,0},{4,2},{6,4},{8,6},{10,8},{12,10},{14,12},{16,14},{18,16},{20... | collective-permute-start | bytes 104 | tf_op jit(solution)/shard_map/ppermute | solution.py:27
  215.5 7.4 %collective-permute-start.27 = (f32[8,1]{1,0:T(8,128)S(1)}, f32[8,1]{1,0:T(8,128)S(1)}, u32[]{:S(2)}, u32[]{:S(2)}) collective-permute-start(f32[8,1]{1,0:T(8,128)S(1)} %get-tuple-element.9), channel_id=1, source_target_pairs={{0,2},{2,4},{4,6},{6,8},{8,10},{10,12},{12,14},{14,16},{16,18},{18... | collective-permute-start | bytes 104 | tf_op jit(solution)/shard_map/ppermute | solution.py:26
  223.3 12.0 %collective-permute-start.32 = (f32[8,16384]{1,0:T(8,128)S(1)}, f32[8,16384]{1,0:T(8,128)S(1)}, u32[]{:S(2)}, u32[]{:S(2)}) collective-permute-start(f32[8,16384]{1,0:T(8,128)S(1)} %fusion.32), channel_id=1, source_target_pairs={{0,1},{1,0},{2,3},{3,2},{4,5},{5,4},{6,7},{7,6},{8,9},{9,8},{10,11... | collective-permute-start | bytes 1572872 | tf_op jit(solution)/shard_map/ppermute | solution.py:16
  226.6 8.5 %collective-permute-start.31 = (f32[8,1]{1,0:T(8,128)S(1)}, f32[8,1]{1,0:T(8,128)S(1)}, u32[]{:S(2)}, u32[]{:S(2)}) collective-permute-start(f32[8,1]{1,0:T(8,128)S(1)} %get-tuple-element.8), channel_id=1, source_target_pairs={{2,0},{4,2},{6,4},{8,6},{10,8},{12,10},{14,12},{16,14},{18,16},{20... | collective-permute-start | bytes 104 | tf_op jit(solution)/shard_map/ppermute | solution.py:27
  227.9 7.4 %collective-permute-start.30 = (f32[8,1]{1,0:T(8,128)S(1)}, f32[8,1]{1,0:T(8,128)S(1)}, u32[]{:S(2)}, u32[]{:S(2)}) collective-permute-start(f32[8,1]{1,0:T(8,128)S(1)} %get-tuple-element.7), channel_id=1, source_target_pairs={{0,2},{2,4},{4,6},{6,8},{8,10},{10,12},{12,14},{14,16},{16,18},{18... | collective-permute-start | bytes 104 | tf_op jit(solution)/shard_map/ppermute | solution.py:26
Sparse Core Ops, SparseCore 0:
  10.5 83.2 all-gather.1
  237.9 237.1 reduce-scatter.1
